TPU v7x, 256 devices: a whole 4x4x8 slice. The times are simulated.
256 devices in a mesh: blk: 16 (over z, x_lo), mode: 16 (over y, x_hi, core).
Axes of the slice: x: 4 (x_hi: 2, x_lo: 2; x = x_hi * 2 + x_lo), y: 4, z: 8, core: 2. Of those that a mesh axis runs over, the one named last changes fastest.
Arguments:
- chaos_field: float32 [448, 65536], P('mode', 'blk'), may hold values from -6 to 6
- kl_field: float32 [13, 65536], P(None, 'blk'), may hold values from -1.6 to 4, as said below
- partner: int32 [12, 2, 448], P(None, None, 'mode'), may hold values from 0 to 447, each once within a row
- chaos_coef: float32 [12, 2, 448], P(None, None, 'mode'), may hold values from 0.5 to 2
- cell_count: int32 [16], P('blk'), may hold values from 2048 to 4096, as said below
- face_count: int32 [16, 4], P('blk'), may hold values from 0 to 128, as said below
- face_cells: int32 [16, 4, 128], P('blk'), may hold values from 0 to 4095, as said below
Outputs:
- applied: float32 [448, 65536], P('mode', 'blk')
Inputs may be any that keep to these rules, and one draw needn't show every extreme that they name: A block's live cells are its first cell_count cells, a whole number of rows of 128; some block is full. `face_count`: slots are the neighbouring blocks at offsets -2, -1, +1, +2 of the block index; a pair of blocks has the same count seen from either side, and 0 where the neighbour does not exist. `face_cells`: entry f of a slot pairs with entry f of the neighbour's opposite slot; entries below the count name live cells. `kl_field`: row 0 lies in 0.5 to 4.
All inputs are finite; a program needn't handle non-finite values.
Results may differ from a plain program's by a relative error of at most 0.000068.
Values sent between devices are 32-bit elements; how exact they have to be, the bound alone decides.
No kernel may reach another device: no remote copies, remote signals or barrier semaphores. Data moves between devices by JAX's collectives and lax.ppermute only.
A program may use at most 64 MiB of HBM per device.

v0:
```python
import jax
import jax.numpy as jnp
from jax import lax
from jax.sharding import PartitionSpec as P

GZ = 128
SLOT_OFFSETS = (-2, -1, 1, 2)
HIGHEST = lax.Precision.HIGHEST


def shifted(value, axis, steps):
    count = lax.axis_size(axis)
    first, last = (max(0, -steps), min(count, count - steps))
    return lax.ppermute(value, axis, [(source, source + steps) for source in range(first, last)])


def grid_terms(values, conduct, alive_grid):
    down_coef = (
        0.5
        * (conduct[..., 1:, :] + conduct[..., :-1, :])
        * (alive_grid[..., 1:, :] * alive_grid[..., :-1, :])
    )
    down_step = down_coef * (values[..., :-1, :] - values[..., 1:, :])
    side_coef = (
        0.5
        * (conduct[..., :, 1:] + conduct[..., :, :-1])
        * (alive_grid[..., :, 1:] * alive_grid[..., :, :-1])
    )
    side_step = side_coef * (values[..., :, :-1] - values[..., :, 1:])
    leading = [(0, 0)] * (values.ndim - 2)
    result = jnp.pad(down_step, leading + [(0, 1), (0, 0)]) - jnp.pad(
        down_step, leading + [(1, 0), (0, 0)]
    )
    return (
        result
        + jnp.pad(side_step, leading + [(0, 0), (0, 1)])
        - jnp.pad(side_step, leading + [(0, 0), (1, 0)])
    )


def operator_terms(values, conduct, alive_grid, own_flat, face_coef, cells_here):
    modes_here = values.shape[0]
    inside = values[:, :cells_here]
    grid_values = inside.reshape(modes_here, alive_grid.shape[0], alive_grid.shape[1])
    grid_part = grid_terms(grid_values, conduct.reshape(alive_grid.shape), alive_grid).reshape(
        modes_here, cells_here
    )
    own_values = jnp.take(inside, own_flat, axis=1)
    face_part = face_coef[None, :] * (own_values - values[:, cells_here:])
    return (grid_part, face_part)


def neighbour_faces(outgoing):
    pieces = []
    for slot_index, offset in enumerate(SLOT_OFFSETS):
        pieces.append(shifted(outgoing[:, 3 - slot_index], "blk", -offset))
    return jnp.stack(pieces, axis=1)


def per_device(chaos_field, kl_field, partner, chaos_coef, cell_count, face_count, face_cells):
    modes_here, cells_here = chaos_field.shape
    rows_grid = cells_here // GZ
    alive_flag = (lax.iota(jnp.int32, cells_here) < cell_count[0]).astype(jnp.float32)
    alive_grid = alive_flag.reshape(rows_grid, GZ)
    masked = chaos_field * alive_flag[None, :]
    face_limit = face_cells.shape[2]
    own_flat = face_cells[0].reshape(-1)
    face_alive = (
        (lax.iota(jnp.int32, face_limit)[None, :] < face_count[0][:, None])
        .astype(jnp.float32)
        .reshape(-1)
    )
    own_conduct = jnp.take(kl_field, own_flat, axis=1)
    outgoing = jnp.concatenate([jnp.take(masked, own_flat, axis=1), own_conduct], axis=0)
    outgoing = outgoing.reshape(outgoing.shape[0], 4, face_limit)
    arrived = neighbour_faces(outgoing)
    arrived = arrived.reshape(arrived.shape[0], 4 * face_limit)
    remote_field = arrived[:modes_here]
    remote_conduct = arrived[modes_here:]
    face_coefs = 0.5 * (own_conduct + remote_conduct) * face_alive[None, :]
    extended = jnp.concatenate([masked, remote_field], axis=1)
    all_modes = modes_here * lax.axis_size("mode")
    mode_ids = lax.iota(jnp.int32, all_modes)
    mixing_rows = jnp.sum(
        jnp.where(partner[:, :, :, None] == mode_ids, chaos_coef[:, :, :, None], 0.0), axis=1
    )
    random_terms = mixing_rows.shape[0]
    grid_zero, face_zero = operator_terms(
        extended, kl_field[0], alive_grid, own_flat, face_coefs[0], cells_here
    )
    own_term = grid_zero.at[:, own_flat].add(face_zero)
    starting = (
        jnp.zeros((modes_here, cells_here), jnp.float32),
        jnp.zeros((modes_here, 4 * face_limit), jnp.float32),
    )
    portion = lax.all_gather(extended, "mode", axis=0, tiled=True)

    def one_term(kl_index, partial_value):
        mixed_part = jnp.dot(
            mixing_rows[kl_index], portion, precision=HIGHEST, preferred_element_type=jnp.float32
        )
        grid_part, face_part = operator_terms(
            mixed_part,
            kl_field[kl_index + 1],
            alive_grid,
            own_flat,
            face_coefs[kl_index + 1],
            cells_here,
        )
        return (partial_value[0] + grid_part, partial_value[1] + face_part)

    grid_sum, face_sum = lax.fori_loop(0, random_terms, one_term, starting)
    summed = grid_sum.at[:, own_flat].add(face_sum) + own_term
    return summed * alive_flag[None, :]


def solution(mesh):
    in_specs = (
        P("mode", "blk"),
        P(None, "blk"),
        P(None, None, "mode"),
        P(None, None, "mode"),
        P("blk"),
        P("blk", None),
        P("blk", None, None),
    )
    out_specs = P("mode", "blk")
    return jax.shard_map(
        per_device, mesh=mesh, in_specs=in_specs, out_specs=out_specs, check_vma=False
    )
```

profile of v0, /device:TPU:1, one launch (start us, length us, event | category | flops | bytes accessed | tf_op | source)
XLA Modules:
  0.0 323.9 jit_solution(10393485028300684983)
XLA Ops:
  9.2 1.1 broadcast_multiply_fusion.1
  11.0 1.0 gather_fusion.2
  13.6 1.0 gather_fusion.1
  15.9 4.4 %collective-permute-start = (f32[41,128]{1,0:T(8,128)S(1)}, f32[41,128]{1,0:T(8,128)S(1)}, u32[]{:S(2)}, u32[]{:S(2)}) collective-permute-start(f32[41,128]{1,0:T(8,128)S(1)} %bitcast.99), channel_id=1, source_target_pairs={{0,32},{16,48},{32,64},{48,80},{64,96},{80,112},{96,128},{112,144}... | collective-permute-start | bytes 62984 | tf_op jit(solution)/shard_map/ppermute | solution.py:14
  20.3 3.1 collective-permute-start.1
  23.4 1.3 collective-permute-start.2
  24.7 1.3 collective-permute-start.3
  26.1 2.1 collective-permute-done.2
  28.2 3.1 collective-permute-done.3
  35.0 2.0 copy.81
  37.1 3.0 fusion.12
  42.3 78.4 %all-gather.3.cloned.1.call-done = f32[16,28,4608]{2,1,0:T(8,128)} async-done(((f32[1,28,4608]{2,1,0:T(8,128)}), f32[16,28,4608]{2,1,0:T(8,128)}) %all-gather.3.cloned.1.call-update) | async-done | bytes 8257552 | tf_op jit(solution)/shard_map/all_gather | solution.py:96
  120.7 9.2 %reshape.167 = f32[448,4608]{1,0:T(8,128)} reshape(f32[16,28,4608]{2,1,0:T(8,128)} %all-gather.3.cloned.1.call-done) | data formatting | bytes 16515072
  129.9 171.5 %while.18 = (s32[]{:T(128)}, f32[28,4096]{1,0:T(8,128)}, f32[28,512]{1,0:T(8,128)S(1)}, f32[13,4096]{1,0:T(8,128)S(1)}, f32[31,128]{1,0:T(8,128)}, /*index=5*/f3...) while((s32[]{:T(128)}, f32[28,4096]{1,0:T(8,128)}, ...), condition=%wide.region_2.4_spmd.clone, body=%wide.region_1.3_spmd.clone.sunk | while | flops 694757632 | bytes 20811360 | solution.py:112
  130.8 7.1 %fusion.31 = f32[28,4608]{1,0:T(8,128)S(1)} fusion(f32[448,4608]{1,0:T(8,128)} %get-tuple-element.445, f32[12,28,448]{2,1,0:T(8,128)} %get-tuple-element.444, s32[]{:T(128)} %get-tuple-element.424), kind=kOutput, calls=%fused_computation.13.clone.1 | convolution fusion | flops 693633024 | bytes 8839680 | tf_op jit(solution)/shard_map/while/body/eval_jaxpr/dot_general | solution.py:99
  142.0 1.0 gather_fusion
  144.1 7.1 %fusion.31 = f32[28,4608]{1,0:T(8,128)S(1)} fusion(f32[448,4608]{1,0:T(8,128)} %get-tuple-element.445, f32[12,28,448]{2,1,0:T(8,128)} %get-tuple-element.444, s32[]{:T(128)} %get-tuple-element.424), kind=kOutput, calls=%fused_computation.13.clone.1 | convolution fusion | flops 693633024 | bytes 8839680 | tf_op jit(solution)/shard_map/while/body/eval_jaxpr/dot_general | solution.py:99
  153.1 1.9 select_add_fusion.2
  156.4 1.0 gather_fusion
  158.5 7.1 %fusion.31 = f32[28,4608]{1,0:T(8,128)S(1)} fusion(f32[448,4608]{1,0:T(8,128)} %get-tuple-element.445, f32[12,28,448]{2,1,0:T(8,128)} %get-tuple-element.444, s32[]{:T(128)} %get-tuple-element.424), kind=kOutput, calls=%fused_computation.13.clone.1 | convolution fusion | flops 693633024 | bytes 8839680 | tf_op jit(solution)/shard_map/while/body/eval_jaxpr/dot_general | solution.py:99
  167.5 1.9 select_add_fusion.2
  170.8 1.0 gather_fusion
  172.9 7.1 %fusion.31 = f32[28,4608]{1,0:T(8,128)S(1)} fusion(f32[448,4608]{1,0:T(8,128)} %get-tuple-element.445, f32[12,28,448]{2,1,0:T(8,128)} %get-tuple-element.444, s32[]{:T(128)} %get-tuple-element.424), kind=kOutput, calls=%fused_computation.13.clone.1 | convolution fusion | flops 693633024 | bytes 8839680 | tf_op jit(solution)/shard_map/while/body/eval_jaxpr/dot_general | solution.py:99
  181.9 1.9 select_add_fusion.2
  185.2 1.0 gather_fusion
  187.3 7.1 %fusion.31 = f32[28,4608]{1,0:T(8,128)S(1)} fusion(f32[448,4608]{1,0:T(8,128)} %get-tuple-element.445, f32[12,28,448]{2,1,0:T(8,128)} %get-tuple-element.444, s32[]{:T(128)} %get-tuple-element.424), kind=kOutput, calls=%fused_computation.13.clone.1 | convolution fusion | flops 693633024 | bytes 8839680 | tf_op jit(solution)/shard_map/while/body/eval_jaxpr/dot_general | solution.py:99
  196.3 1.9 select_add_fusion.2
  199.6 1.0 gather_fusion
  201.7 7.1 %fusion.31 = f32[28,4608]{1,0:T(8,128)S(1)} fusion(f32[448,4608]{1,0:T(8,128)} %get-tuple-element.445, f32[12,28,448]{2,1,0:T(8,128)} %get-tuple-element.444, s32[]{:T(128)} %get-tuple-element.424), kind=kOutput, calls=%fused_computation.13.clone.1 | convolution fusion | flops 693633024 | bytes 8839680 | tf_op jit(solution)/shard_map/while/body/eval_jaxpr/dot_general | solution.py:99
  210.7 1.9 select_add_fusion.2
  214.0 1.0 gather_fusion
  216.0 7.1 %fusion.31 = f32[28,4608]{1,0:T(8,128)S(1)} fusion(f32[448,4608]{1,0:T(8,128)} %get-tuple-element.445, f32[12,28,448]{2,1,0:T(8,128)} %get-tuple-element.444, s32[]{:T(128)} %get-tuple-element.424), kind=kOutput, calls=%fused_computation.13.clone.1 | convolution fusion | flops 693633024 | bytes 8839680 | tf_op jit(solution)/shard_map/while/body/eval_jaxpr/dot_general | solution.py:99
  225.0 1.9 select_add_fusion.2
  228.3 1.0 gather_fusion
  230.4 7.1 %fusion.31 = f32[28,4608]{1,0:T(8,128)S(1)} fusion(f32[448,4608]{1,0:T(8,128)} %get-tuple-element.445, f32[12,28,448]{2,1,0:T(8,128)} %get-tuple-element.444, s32[]{:T(128)} %get-tuple-element.424), kind=kOutput, calls=%fused_computation.13.clone.1 | convolution fusion | flops 693633024 | bytes 8839680 | tf_op jit(solution)/shard_map/while/body/eval_jaxpr/dot_general | solution.py:99
  239.4 1.9 select_add_fusion.2
  242.7 1.0 gather_fusion
  244.8 7.1 %fusion.31 = f32[28,4608]{1,0:T(8,128)S(1)} fusion(f32[448,4608]{1,0:T(8,128)} %get-tuple-element.445, f32[12,28,448]{2,1,0:T(8,128)} %get-tuple-element.444, s32[]{:T(128)} %get-tuple-element.424), kind=kOutput, calls=%fused_computation.13.clone.1 | convolution fusion | flops 693633024 | bytes 8839680 | tf_op jit(solution)/shard_map/while/body/eval_jaxpr/dot_general | solution.py:99
  253.8 1.9 select_add_fusion.2
  259.2 7.1 %fusion.31 = f32[28,4608]{1,0:T(8,128)S(1)} fusion(f32[448,4608]{1,0:T(8,128)} %get-tuple-element.445, f32[12,28,448]{2,1,0:T(8,128)} %get-tuple-element.444, s32[]{:T(128)} %get-tuple-element.424), kind=kOutput, calls=%fused_computation.13.clone.1 | convolution fusion | flops 693633024 | bytes 8839680 | tf_op jit(solution)/shard_map/while/body/eval_jaxpr/dot_general | solution.py:99
  268.2 1.9 select_add_fusion.2
  273.6 7.1 %fusion.31 = f32[28,4608]{1,0:T(8,128)S(1)} fusion(f32[448,4608]{1,0:T(8,128)} %get-tuple-element.445, f32[12,28,448]{2,1,0:T(8,128)} %get-tuple-element.444, s32[]{:T(128)} %get-tuple-element.424), kind=kOutput, calls=%fused_computation.13.clone.1 | convolution fusion | flops 693633024 | bytes 8839680 | tf_op jit(solution)/shard_map/while/body/eval_jaxpr/dot_general | solution.py:99
  282.6 1.9 select_add_fusion.2
  288.0 7.1 %fusion.31 = f32[28,4608]{1,0:T(8,128)S(1)} fusion(f32[448,4608]{1,0:T(8,128)} %get-tuple-element.445, f32[12,28,448]{2,1,0:T(8,128)} %get-tuple-element.444, s32[]{:T(128)} %get-tuple-element.424), kind=kOutput, calls=%fused_computation.13.clone.1 | convolution fusion | flops 693633024 | bytes 8839680 | tf_op jit(solution)/shard_map/while/body/eval_jaxpr/dot_general | solution.py:99
  297.0 1.9 select_add_fusion.2
  302.5 3.0 copy.82
  305.6 2.4 bitcast_add_fusion
  308.0 7.6 %scatter_fusion = f32[28,4096]{0,1:T(8,128)S(1)} fusion(f32[28,4096]{0,1:T(8,128)S(1)} %bitcast_add_fusion, s32[1024]{0:T(1024)S(1)} %bitcast.104, f32[1024,28]{1,0:T(8,128)S(1)} %copy.84), kind=kCustom, calls=%fused_computation.3 | custom fusion | flops 28672 | bytes 348160 | tf_op jit(solution)/shard_map/add | solution.py:113
  (317 shorter events, 69.0 us)
Async XLA Ops:
  6.5 114.1 %all-gather.3.cloned.1.call-start = ((), (), s32[]{:S(2)}) async-start(), calls=%async_computation | async-start | bytes 10027008 | tf_op jit(solution)/shard_map/all_gather | solution.py:96
  7.9 6.7 %copy-start.7 = (pred[512]{0:T(512)(128)(4,1)}, pred[512]{0:T(512)(128)(4,1)S(1)}, u32[]{:S(2)}) copy-start(pred[512]{0:T(512)(128)(4,1)S(1)} %compare_and_fusion.1) | copy-start | bytes 1540
  8.6 0.6 copy-start.3
  10.3 2.6 copy-start.1
  10.3 2.6 copy-start
  12.9 1.9 copy-start.5
  14.8 17.8 %copy-start.9 = (s32[12,2,28]{2,1,0:T(2,128)S(1)}, s32[12,2,28]{2,1,0:T(2,128)}, u32[]{:S(2)}) copy-start(s32[12,2,28]{2,1,0:T(2,128)} %param.13) | copy-start | bytes 8068
  14.8 18.0 %copy-start.10 = (f32[12,2,28]{2,1,0:T(2,128)S(1)}, f32[12,2,28]{2,1,0:T(2,128)}, u32[]{:S(2)}) copy-start(f32[12,2,28]{2,1,0:T(2,128)} %param.14) | copy-start | bytes 8068
  15.9 10.1 %collective-permute-start = (f32[41,128]{1,0:T(8,128)S(1)}, f32[41,128]{1,0:T(8,128)S(1)}, u32[]{:S(2)}, u32[]{:S(2)}) collective-permute-start(f32[41,128]{1,0:T(8,128)S(1)} %bitcast.99), channel_id=1, source_target_pairs={{0,32},{16,48},{32,64},{48,80},{64,96},{80,112},{96,128},{112,144}... | collective-permute-start | bytes 62984 | tf_op jit(solution)/shard_map/ppermute | solution.py:14
  20.3 5.8 %collective-permute-start.1 = (f32[41,128]{1,0:T(8,128)S(1)}, f32[41,128]{1,0:T(8,128)S(1)}, u32[]{:S(2)}, u32[]{:S(2)}) collective-permute-start(f32[41,128]{1,0:T(8,128)S(1)} %bitcast.100), channel_id=1, source_target_pairs={{0,16},{16,32},{32,48},{48,64},{64,80},{80,96},{96,112},{112,128},... | collective-permute-start | bytes 62984 | tf_op jit(solution)/shard_map/ppermute | solution.py:14
  23.4 4.7 %collective-permute-start.2 = (f32[41,128]{1,0:T(8,128)S(1)}, f32[41,128]{1,0:T(8,128)S(1)}, u32[]{:S(2)}, u32[]{:S(2)}) collective-permute-start(f32[41,128]{1,0:T(8,128)S(1)} %bitcast.101), channel_id=1, source_target_pairs={{16,0},{32,16},{48,32},{64,48},{80,64},{96,80},{112,96},{128,112},... | collective-permute-start | bytes 62984 | tf_op jit(solution)/shard_map/ppermute | solution.py:14
  24.7 6.5 %collective-permute-start.3 = (f32[41,128]{1,0:T(8,128)S(1)}, f32[41,128]{1,0:T(8,128)S(1)}, u32[]{:S(2)}, u32[]{:S(2)}) collective-permute-start(f32[41,128]{1,0:T(8,128)S(1)} %bitcast.102), channel_id=1, source_target_pairs={{32,0},{48,16},{64,32},{80,48},{96,64},{112,80},{128,96},{144,112}... | collective-permute-start | bytes 62984 | tf_op jit(solution)/shard_map/ppermute | solution.py:14
  31.7 2.1 slice-start
  34.7 2.3 copy-start.6
  34.7 2.3 copy-start.11
  35.0 5.3 %copy-start.8 = (pred[512]{0:T(512)(128)(4,1)S(1)}, pred[512]{0:T(512)(128)(4,1)}, u32[]{:S(2)}) copy-start(pred[512]{0:T(512)(128)(4,1)} %copy-done.7) | copy-start | bytes 1540
  42.3 87.6 %copy-start.2 = (s32[1,4,128]{2,1,0:T(4,128)S(1)}, s32[1,4,128]{2,1,0:T(4,128)}, u32[]{:S(2)}) copy-start(s32[1,4,128]{2,1,0:T(4,128)} %param.17) | copy-start | bytes 6148
  308.0 8.2 %copy-start.4 = (f32[4096]{0:T(1024)S(1)}, f32[4096]{0:T(1024)}, u32[]{:S(2)}) copy-start(f32[4096]{0:T(1024)} %copy-done.3) | copy-start | bytes 49156
Sparse Core Ops, SparseCore 0:
  32.7 87.9 all-gather.2
where the time goes:
time: 328 us; the launch traced here: 324 us
  matrix products  85.4 us (26%)
  waiting for transfers between devices  83.6 us (25%)
  other arithmetic  69.2 us (21%)
  local copies, waits for them, and re-layouts  59.3 us (18%)
  between operations  14.5 us (4%)
  starting transfers between devices  10.1 us (3%)
    dot_general x12, matrix products, one_term(): jnp.dot(mixing_rows[kl_index], portion, precision=HIGHEST, preferred_elem...  85.4 us
    all_gather x1, waiting for transfers between devices, per_device(): portion = lax.all_gather(extended, 'mode', axis=0, tiled=True)  78.4 us
    add x24, other arithmetic, one_term(): return (partial_value[0] + grid_part, partial_value[1] + face_part)  22.1 us
    gather x24, local copies, waits for them, and re-layouts, operator_terms(): own_values = jnp.take(inside, own_flat, axis=1)  13.8 us
    unnamed x34, local copies, waits for them, and re-layouts  11.7 us
    mul x26, other arithmetic, grid_terms(): 0.5 * (conduct[..., 1:, :] + conduct[..., :-1, :])  10.8 us
    mul x13, other arithmetic, grid_terms(): 0.5 * (conduct[..., :, 1:] + conduct[..., :, :-1])  10.2 us
    ppermute x4, starting transfers between devices, shifted(): lax.ppermute(value, axis, [(source, source + steps) for source in range(f...  10.1 us
  transfers between devices with their start and end apart: 5, of which 3 were waited for; matrix products, arithmetic and copies ran while one was open for 3% of the time, Pallas kernels for 0%

commit v1 on v0

--- a/solution.py
+++ b/solution.py
@@ -93,7 +93,9 @@
         jnp.zeros((modes_here, cells_here), jnp.float32),
         jnp.zeros((modes_here, 4 * face_limit), jnp.float32),
     )
-    portion = lax.all_gather(extended, "mode", axis=0, tiled=True)
+    portion = jnp.concatenate(
+        lax.all_to_all(jnp.stack([extended] * lax.axis_size("mode")), "mode", 0, 0), axis=0
+    )
 
     def one_term(kl_index, partial_value):
         mixed_part = jnp.dot(

time: 328 us -> 348 us (1.061)
  waiting for transfers between devices: 83.6 us -> 103 us
  between operations: 14.5 us -> 1.12 us
  starting transfers between devices: 10.1 us -> 19.5 us
  local copies, waits for them, and re-layouts: 59.3 us -> 64.1 us
    all_to_all x0 -> x1, waiting for transfers between devices: none -> 97.6 us  [per_device(): lax.all_to_all(jnp.stack([extended] * lax.axis_size('mode')), 'mode', 0, 0)]
    all_gather x1 -> x0, waiting for transfers between devices: 78.4 us -> none  [per_device(): portion = lax.all_gather(extended, 'mode', axis=0, tiled=True)]
    all_to_all x0 -> x1, starting transfers between devices: none -> 9.44 us  [per_device(): lax.all_to_all(jnp.stack([extended] * lax.axis_size('mode')), 'mode', 0, 0)]
    unnamed x34 -> x33, local copies, waits for them, and re-layouts: 11.7 us -> 2.45 us
    reshape x0 -> x1, local copies, waits for them, and re-layouts: none -> 9.25 us  [per_device(): jnp.concatenate(lax.all_to_all(jnp.stack([extended] * lax.axis_size('mode...]
    another operation x1 -> x2, local copies, waits for them, and re-layouts: 0.21 us -> 5.01 us  [the longest x1 4.8 us: per_device(): jnp.stack([extended] * lax.axis_size('mode'))]
where the time goes in v1:
time: 348 us; the launch traced here: 343 us
  waiting for transfers between devices  103 us (30%)
  matrix products  85.4 us (25%)
  other arithmetic  68.4 us (20%)
  local copies, waits for them, and re-layouts  64.1 us (18%)
  starting transfers between devices  19.5 us (6%)
    all_to_all x1, waiting for transfers between devices, per_device(): lax.all_to_all(jnp.stack([extended] * lax.axis_size('mode')), 'mode', 0, 0)  97.6 us
    dot_general x12, matrix products, one_term(): jnp.dot(mixing_rows[kl_index], portion, precision=HIGHEST, preferred_elem...  85.4 us
    add x24, other arithmetic, one_term(): return (partial_value[0] + grid_part, partial_value[1] + face_part)  22.1 us
    gather x24, local copies, waits for them, and re-layouts, operator_terms(): own_values = jnp.take(inside, own_flat, axis=1)  13.8 us
    mul x26, other arithmetic, grid_terms(): 0.5 * (conduct[..., 1:, :] + conduct[..., :-1, :])  10.8 us
    mul x13, other arithmetic, grid_terms(): 0.5 * (conduct[..., :, 1:] + conduct[..., :, :-1])  10.2 us
    ppermute x4, starting transfers between devices, shifted(): lax.ppermute(value, axis, [(source, source + steps) for source in range(f...  10.1 us
    all_to_all x1, starting transfers between devices, per_device(): lax.all_to_all(jnp.stack([extended] * lax.axis_size('mode')), 'mode', 0, 0)  9.44 us
  transfers between devices with their start and end apart: 5, of which 3 were waited for; matrix products, arithmetic and copies ran while one was open for 3% of the time, Pallas kernels for 0%

profile of v1, /device:TPU:1, one launch (start us, length us, event | category | flops | bytes accessed | tf_op | source)
XLA Modules:
  0.0 343.1 jit_solution(16387069374871193259)
XLA Ops:
  2.6 1.1 broadcast_multiply_fusion.1
  7.0 1.0 gather_fusion.1
  9.3 4.4 %collective-permute-start = (f32[41,128]{1,0:T(8,128)S(1)}, f32[41,128]{1,0:T(8,128)S(1)}, u32[]{:S(2)}, u32[]{:S(2)}) collective-permute-start(f32[41,128]{1,0:T(8,128)S(1)} %bitcast.97), channel_id=1, source_target_pairs={{0,32},{16,48},{32,64},{48,80},{64,96},{80,112},{96,128},{112,144}... | collective-permute-start | bytes 62984 | tf_op jit(solution)/shard_map/ppermute | solution.py:14
  13.7 3.1 collective-permute-start.1
  16.9 1.3 collective-permute-start.2
  18.2 1.3 collective-permute-start.3
  19.5 2.1 collective-permute-done.2
  21.6 3.1 collective-permute-done.3
  25.2 4.8 %stack.17 = f32[16,28,4608]{2,1,0:T(8,128)} broadcast(f32[28,4608]{1,0:T(8,128)S(1)} %pad_maximum_fusion), dimensions={1,2} | broadcast | bytes 8773632 | tf_op jit(solution)/shard_map/stack | solution.py:97
  30.0 9.4 %all-to-all-start = ((f32[16,28,4608]{2,1,0:T(8,128)}), f32[16,28,4608]{2,1,0:T(8,128)}, u32[]{:S(2)}, u32[]{:S(2)}) async-start(f32[16,28,4608]{2,1,0:T(8,128)} %stack.17), calls=%async_computation | async-start | bytes 18874368 | tf_op jit(solution)/shard_map/all_to_all | solution.py:97
  41.8 2.0 copy.82
  43.9 3.0 fusion.12
  49.1 97.6 %all-to-all-done = f32[16,28,4608]{2,1,0:T(8,128)} async-done(((f32[16,28,4608]{2,1,0:T(8,128)}), f32[16,28,4608]{2,1,0:T(8,128)}, u32[]{:S(2)}, u32[]{:S(2)}) %all-to-all-start) | async-done | bytes 8257568 | tf_op jit(solution)/shard_map/all_to_all | solution.py:97
  146.7 9.3 %reshape.135 = f32[448,4608]{1,0:T(8,128)} reshape(f32[16,28,4608]{2,1,0:T(8,128)} %all-to-all-done) | data formatting | bytes 16515072 | tf_op jit(solution)/shard_map/reshape | solution.py:96
  155.9 171.5 %while.18 = (s32[]{:T(128)}, f32[28,4096]{1,0:T(8,128)}, f32[28,512]{1,0:T(8,128)S(1)}, f32[13,4096]{1,0:T(8,128)S(1)}, f32[31,128]{1,0:T(8,128)}, /*index=5*/f3...) while((s32[]{:T(128)}, f32[28,4096]{1,0:T(8,128)}, ...), condition=%wide.region_2.4_spmd.clone, body=%wide.region_1.3_spmd.clone.sunk | while | flops 694757632 | bytes 20811360 | solution.py:114
  156.8 7.1 %fusion.31 = f32[28,4608]{1,0:T(8,128)S(1)} fusion(f32[448,4608]{1,0:T(8,128)} %get-tuple-element.445, f32[12,28,448]{2,1,0:T(8,128)} %get-tuple-element.444, s32[]{:T(128)} %get-tuple-element.424), kind=kOutput, calls=%fused_computation.13.clone.1 | convolution fusion | flops 693633024 | bytes 8839680 | tf_op jit(solution)/shard_map/while/body/eval_jaxpr/dot_general | solution.py:101
  168.1 1.0 gather_fusion
  170.1 7.1 %fusion.31 = f32[28,4608]{1,0:T(8,128)S(1)} fusion(f32[448,4608]{1,0:T(8,128)} %get-tuple-element.445, f32[12,28,448]{2,1,0:T(8,128)} %get-tuple-element.444, s32[]{:T(128)} %get-tuple-element.424), kind=kOutput, calls=%fused_computation.13.clone.1 | convolution fusion | flops 693633024 | bytes 8839680 | tf_op jit(solution)/shard_map/while/body/eval_jaxpr/dot_general | solution.py:101
  179.1 1.9 select_add_fusion.2
  182.4 1.0 gather_fusion
  184.5 7.1 %fusion.31 = f32[28,4608]{1,0:T(8,128)S(1)} fusion(f32[448,4608]{1,0:T(8,128)} %get-tuple-element.445, f32[12,28,448]{2,1,0:T(8,128)} %get-tuple-element.444, s32[]{:T(128)} %get-tuple-element.424), kind=kOutput, calls=%fused_computation.13.clone.1 | convolution fusion | flops 693633024 | bytes 8839680 | tf_op jit(solution)/shard_map/while/body/eval_jaxpr/dot_general | solution.py:101
  193.5 1.9 select_add_fusion.2
  196.8 1.0 gather_fusion
  198.9 7.1 %fusion.31 = f32[28,4608]{1,0:T(8,128)S(1)} fusion(f32[448,4608]{1,0:T(8,128)} %get-tuple-element.445, f32[12,28,448]{2,1,0:T(8,128)} %get-tuple-element.444, s32[]{:T(128)} %get-tuple-element.424), kind=kOutput, calls=%fused_computation.13.clone.1 | convolution fusion | flops 693633024 | bytes 8839680 | tf_op jit(solution)/shard_map/while/body/eval_jaxpr/dot_general | solution.py:101
  207.9 1.9 select_add_fusion.2
  211.2 1.0 gather_fusion
  213.3 7.1 %fusion.31 = f32[28,4608]{1,0:T(8,128)S(1)} fusion(f32[448,4608]{1,0:T(8,128)} %get-tuple-element.445, f32[12,28,448]{2,1,0:T(8,128)} %get-tuple-element.444, s32[]{:T(128)} %get-tuple-element.424), kind=kOutput, calls=%fused_computation.13.clone.1 | convolution fusion | flops 693633024 | bytes 8839680 | tf_op jit(solution)/shard_map/while/body/eval_jaxpr/dot_general | solution.py:101
  222.3 1.9 select_add_fusion.2
  227.7 7.1 %fusion.31 = f32[28,4608]{1,0:T(8,128)S(1)} fusion(f32[448,4608]{1,0:T(8,128)} %get-tuple-element.445, f32[12,28,448]{2,1,0:T(8,128)} %get-tuple-element.444, s32[]{:T(128)} %get-tuple-element.424), kind=kOutput, calls=%fused_computation.13.clone.1 | convolution fusion | flops 693633024 | bytes 8839680 | tf_op jit(solution)/shard_map/while/body/eval_jaxpr/dot_general | solution.py:101
  236.7 1.9 select_add_fusion.2
  242.1 7.1 %fusion.31 = f32[28,4608]{1,0:T(8,128)S(1)} fusion(f32[448,4608]{1,0:T(8,128)} %get-tuple-element.445, f32[12,28,448]{2,1,0:T(8,128)} %get-tuple-element.444, s32[]{:T(128)} %get-tuple-element.424), kind=kOutput, calls=%fused_computation.13.clone.1 | convolution fusion | flops 693633024 | bytes 8839680 | tf_op jit(solution)/shard_map/while/body/eval_jaxpr/dot_general | solution.py:101
  251.1 1.9 select_add_fusion.2
  256.4 7.1 %fusion.31 = f32[28,4608]{1,0:T(8,128)S(1)} fusion(f32[448,4608]{1,0:T(8,128)} %get-tuple-element.445, f32[12,28,448]{2,1,0:T(8,128)} %get-tuple-element.444, s32[]{:T(128)} %get-tuple-element.424), kind=kOutput, calls=%fused_computation.13.clone.1 | convolution fusion | flops 693633024 | bytes 8839680 | tf_op jit(solution)/shard_map/while/body/eval_jaxpr/dot_general | solution.py:101
  265.4 1.9 select_add_fusion.2
  270.8 7.1 %fusion.31 = f32[28,4608]{1,0:T(8,128)S(1)} fusion(f32[448,4608]{1,0:T(8,128)} %get-tuple-element.445, f32[12,28,448]{2,1,0:T(8,128)} %get-tuple-element.444, s32[]{:T(128)} %get-tuple-element.424), kind=kOutput, calls=%fused_computation.13.clone.1 | convolution fusion | flops 693633024 | bytes 8839680 | tf_op jit(solution)/shard_map/while/body/eval_jaxpr/dot_general | solution.py:101
  279.8 1.9 select_add_fusion.2
  285.2 7.1 %fusion.31 = f32[28,4608]{1,0:T(8,128)S(1)} fusion(f32[448,4608]{1,0:T(8,128)} %get-tuple-element.445, f32[12,28,448]{2,1,0:T(8,128)} %get-tuple-element.444, s32[]{:T(128)} %get-tuple-element.424), kind=kOutput, calls=%fused_computation.13.clone.1 | convolution fusion | flops 693633024 | bytes 8839680 | tf_op jit(solution)/shard_map/while/body/eval_jaxpr/dot_general | solution.py:101
  294.2 1.9 select_add_fusion.2
  297.5 1.0 gather_fusion
  299.6 7.1 %fusion.31 = f32[28,4608]{1,0:T(8,128)S(1)} fusion(f32[448,4608]{1,0:T(8,128)} %get-tuple-element.445, f32[12,28,448]{2,1,0:T(8,128)} %get-tuple-element.444, s32[]{:T(128)} %get-tuple-element.424), kind=kOutput, calls=%fused_computation.13.clone.1 | convolution fusion | flops 693633024 | bytes 8839680 | tf_op jit(solution)/shard_map/while/body/eval_jaxpr/dot_general | solution.py:101
  308.6 1.9 select_add_fusion.2
  311.9 1.0 gather_fusion
  314.0 7.1 %fusion.31 = f32[28,4608]{1,0:T(8,128)S(1)} fusion(f32[448,4608]{1,0:T(8,128)} %get-tuple-element.445, f32[12,28,448]{2,1,0:T(8,128)} %get-tuple-element.444, s32[]{:T(128)} %get-tuple-element.424), kind=kOutput, calls=%fused_computation.13.clone.1 | convolution fusion | flops 693633024 | bytes 8839680 | tf_op jit(solution)/shard_map/while/body/eval_jaxpr/dot_general | solution.py:101
  323.0 1.9 select_add_fusion.2
  326.3 1.0 gather_fusion
  328.6 3.0 copy.83
  331.6 2.4 bitcast_add_fusion
  334.0 7.6 %scatter_fusion = f32[28,4096]{0,1:T(8,128)S(1)} fusion(f32[28,4096]{0,1:T(8,128)S(1)} %bitcast_add_fusion, s32[1024]{0:T(1024)S(1)} %bitcast.102, f32[1024,28]{1,0:T(8,128)S(1)} %copy.85), kind=kCustom, calls=%fused_computation.3 | custom fusion | flops 28672 | bytes 348160 | tf_op jit(solution)/shard_map/add | solution.py:115
  (317 shorter events, 70.2 us)
Async XLA Ops:
  1.4 6.7 %copy-start.7 = (pred[512]{0:T(512)(128)(4,1)}, pred[512]{0:T(512)(128)(4,1)S(1)}, u32[]{:S(2)}) copy-start(pred[512]{0:T(512)(128)(4,1)S(1)} %compare_and_fusion.1) | copy-start | bytes 1540
  2.0 0.6 copy-start.3
  3.7 2.6 copy-start.1
  3.7 2.6 copy-start
  6.4 1.9 copy-start.5
  9.3 10.1 %collective-permute-start = (f32[41,128]{1,0:T(8,128)S(1)}, f32[41,128]{1,0:T(8,128)S(1)}, u32[]{:S(2)}, u32[]{:S(2)}) collective-permute-start(f32[41,128]{1,0:T(8,128)S(1)} %bitcast.97), channel_id=1, source_target_pairs={{0,32},{16,48},{32,64},{48,80},{64,96},{80,112},{96,128},{112,144}... | collective-permute-start | bytes 62984 | tf_op jit(solution)/shard_map/ppermute | solution.py:14
  13.7 5.8 %collective-permute-start.1 = (f32[41,128]{1,0:T(8,128)S(1)}, f32[41,128]{1,0:T(8,128)S(1)}, u32[]{:S(2)}, u32[]{:S(2)}) collective-permute-start(f32[41,128]{1,0:T(8,128)S(1)} %bitcast.98), channel_id=1, source_target_pairs={{0,16},{16,32},{32,48},{48,64},{64,80},{80,96},{96,112},{112,128},... | collective-permute-start | bytes 62984 | tf_op jit(solution)/shard_map/ppermute | solution.py:14
  16.9 4.7 %collective-permute-start.2 = (f32[41,128]{1,0:T(8,128)S(1)}, f32[41,128]{1,0:T(8,128)S(1)}, u32[]{:S(2)}, u32[]{:S(2)}) collective-permute-start(f32[41,128]{1,0:T(8,128)S(1)} %bitcast.99), channel_id=1, source_target_pairs={{16,0},{32,16},{48,32},{64,48},{80,64},{96,80},{112,96},{128,112},... | collective-permute-start | bytes 62984 | tf_op jit(solution)/shard_map/ppermute | solution.py:14
  18.2 6.5 %collective-permute-start.3 = (f32[41,128]{1,0:T(8,128)S(1)}, f32[41,128]{1,0:T(8,128)S(1)}, u32[]{:S(2)}, u32[]{:S(2)}) collective-permute-start(f32[41,128]{1,0:T(8,128)S(1)} %bitcast.100), channel_id=1, source_target_pairs={{32,0},{48,16},{64,32},{80,48},{96,64},{112,80},{128,96},{144,112}... | collective-permute-start | bytes 62984 | tf_op jit(solution)/shard_map/ppermute | solution.py:14
  30.0 9.5 %copy-start.9 = (s32[12,2,28]{2,1,0:T(2,128)S(1)}, s32[12,2,28]{2,1,0:T(2,128)}, u32[]{:S(2)}) copy-start(s32[12,2,28]{2,1,0:T(2,128)} %param.13) | copy-start | bytes 8068
  30.0 9.7 %copy-start.10 = (f32[12,2,28]{2,1,0:T(2,128)S(1)}, f32[12,2,28]{2,1,0:T(2,128)}, u32[]{:S(2)}) copy-start(f32[12,2,28]{2,1,0:T(2,128)} %param.14) | copy-start | bytes 8068
  30.0 116.7 %all-to-all-start = ((f32[16,28,4608]{2,1,0:T(8,128)}), f32[16,28,4608]{2,1,0:T(8,128)}, u32[]{:S(2)}, u32[]{:S(2)}) async-start(f32[16,28,4608]{2,1,0:T(8,128)} %stack.17), calls=%async_computation | async-start | bytes 18874368 | tf_op jit(solution)/shard_map/all_to_all | solution.py:97
  39.4 1.2 slice-start
  41.6 2.2 copy-start.6
  41.6 2.2 copy-start.11
  41.8 5.3 %copy-start.8 = (pred[512]{0:T(512)(128)(4,1)S(1)}, pred[512]{0:T(512)(128)(4,1)}, u32[]{:S(2)}) copy-start(pred[512]{0:T(512)(128)(4,1)} %copy-done.7) | copy-start | bytes 1540
  49.1 106.8 %copy-start.2 = (s32[1,4,128]{2,1,0:T(4,128)S(1)}, s32[1,4,128]{2,1,0:T(4,128)}, u32[]{:S(2)}) copy-start(s32[1,4,128]{2,1,0:T(4,128)} %param.17) | copy-start | bytes 6148
  334.0 8.2 %copy-start.4 = (f32[4096]{0:T(1024)S(1)}, f32[4096]{0:T(1024)}, u32[]{:S(2)}) copy-start(f32[4096]{0:T(1024)} %copy-done.3) | copy-start | bytes 49156
